TPU v7x, 256 devices: a whole 4x4x8 slice. The times are simulated.
256 devices in a mesh: slab: 64 (over y, z, core), grp: 4 (over x).
Axes of the slice: x: 4, y: 4, z: 8, core: 2. Of those that a mesh axis runs over, the one named last changes fastest.
Arguments:
- blocks: bfloat16 [4, 4, 1024, 128, 128], P('grp', None, 'slab'), may hold values from -6 to 6
- coords: int32 [4, 64, 4, 2], P('grp', 'slab'), may hold values from 0 to 15
- counts: int32 [4, 64], P('grp', 'slab'), may hold values from 1 to 4, as said below
- omega1: bfloat16 [1024, 512], replicated, may hold values from -0.1875 to 0.1875
- omega2: bfloat16 [2048, 512], replicated, may hold values from -0.5 to 0.5
- omega3: bfloat16 [2048, 512], replicated, may hold values from -0.125 to 0.125
Outputs:
- core_sketch: float32 [512, 512, 512], P(None, 'slab', 'grp')
Inputs may be any that keep to these rules, and one draw needn't show every extreme that they name: counts[g, s] slots are live in the list of group g on slab s; slots from it on are ignored. Some list holds 4 live slots in every draw.
All inputs are finite; a program needn't handle non-finite values.
Results may differ from a plain program's by a relative error of at most 0.0041.
Values may be sent and summed in bfloat16 or wider, within the bound.
No kernel may reach another device: no remote copies, remote signals or barrier semaphores. Data moves between devices by JAX's collectives and lax.ppermute only.
A program may use at most 128 MiB of HBM per device.

v0:
```python
import functools

import jax
import jax.numpy as jnp
from jax import lax
from jax.experimental import pallas as pl
from jax.experimental.pallas import tpu as pltpu
from jax.sharding import PartitionSpec as P


EDGE = 128
SIDE_Y, SIDE_Z, CORES = 4, 8, 2
CHUNKS, ROWS = 2, 2
LEAVE = (4, 3, 5, 2, 6, 1, 7)
STAGE_LIMIT = 16 << 20
FOLD_LIMIT = (40 << 20, 56 << 20)
VMEM = pl.BlockSpec(memory_space=pltpu.VMEM)


def stage_kernel(omega, out, sem):
    copy = pltpu.make_async_copy(omega, out, sem)
    copy.start()
    copy.wait()


def stage(omega):
    return pl.pallas_call(
        stage_kernel,
        out_shape=jax.ShapeDtypeStruct(omega.shape, omega.dtype),
        in_specs=[pl.BlockSpec(memory_space=pltpu.HBM)],
        out_specs=VMEM,
        scratch_shapes=[pltpu.SemaphoreType.DMA(())],
        compiler_params=pltpu.CompilerParams(vmem_limit_bytes=STAGE_LIMIT),
        name="stage",
    )(omega)


def fold_kernel(count, meta, *refs):
    outs = refs[-3 - count : -3]
    pieces = refs[: -3 - count]
    pieces, (omega2t, omega3) = pieces[:-2], pieces[-2:]
    after, second, acc = refs[-3:]
    rows, rank = acc.shape[0], acc.shape[2]
    slots = pieces[0].shape[0]
    groups = outs[0].shape[2]
    here = lax.rem(lax.div(lax.axis_index("slab"), CORES), SIDE_Z)

    def place_slot(source, piece, slot, spot):
        third = pl.multiple_of(meta[source, 2 * slot + 1] * EDGE, EDGE)
        mode2 = pl.multiple_of(meta[source, 2 * slot] * EDGE, EDGE)
        at = pl.multiple_of(spot * EDGE, EDGE)
        product = jnp.dot(
            piece[slot].reshape(rows * EDGE, EDGE),
            omega3[pl.ds(third, EDGE), :],
            preferred_element_type=jnp.float32,
        ).astype(jnp.bfloat16)
        for row in range(rows):
            after[row, pl.ds(at, EDGE), :] = product[row * EDGE : (row + 1) * EDGE]
        second[:, pl.ds(at, EDGE)] = omega2t[:, pl.ds(mode2, EDGE)]

    sources = list(enumerate(pieces))
    lists = len(sources)
    base = lists
    for order, (source, piece) in enumerate(sources):
        place_slot(source, piece, 0, order)

        def one_slot(slot, carry, source=source, piece=piece, base=base):
            place_slot(source, piece, slot, base + slot - 1)
            return carry

        lax.fori_loop(1, meta[source, 2 * slots], one_slot, 0)
        base = base + meta[source, 2 * slots] - 1

    @pl.when(base % 2 == 1)
    def _():
        at = pl.multiple_of(base * EDGE, EDGE)
        for row in range(rows):
            after[row, pl.ds(at, EDGE), :] = jnp.zeros((EDGE, rank), jnp.bfloat16)
        second[:, pl.ds(at, EDGE)] = jnp.zeros((rank, EDGE), jnp.bfloat16)

    width = rank // groups
    strip = outs[0].shape[4]
    for row in range(rows):
        acc[row] = jnp.dot(
            second[:, : lists * EDGE],
            after[row, : lists * EDGE, :],
            preferred_element_type=jnp.float32,
        )

        def next_pair(pair, carry, row=row):
            at = pl.multiple_of(pair * 2 * EDGE, 2 * EDGE)
            acc[row] += jnp.dot(
                second[:, pl.ds(at, 2 * EDGE)],
                after[row, pl.ds(at, 2 * EDGE), :],
                preferred_element_type=jnp.float32,
            )
            return carry

        lax.fori_loop(lists // 2, (base + 1) // 2, next_pair, 0)
        for step in range(SIDE_Z):
            out, line = (outs[0], step * rows + row) if count == 1 else (outs[step], row)
            there = lax.rem(here + step, SIDE_Z)
            for y in range(SIDE_Y):
                at = pl.multiple_of((y * SIDE_Z + there) * CORES * strip, CORES * strip)
                for group in range(groups):
                    cols = acc[row, pl.ds(at, CORES * strip), group * width : (group + 1) * width]
                    out[y, :, group, line] = cols.reshape(CORES, strip, width).astype(jnp.bfloat16)


def fold(meta, pieces, omega2t, omega3, limit, count, slabs, groups):
    slots, rows = pieces[0].shape[:2]
    rank = omega2t.shape[0]
    depth = groups * slots * EDGE
    form = (SIDE_Y, CORES, groups, rows * SIDE_Z // count, rank // slabs, rank // groups)
    return pl.pallas_call(
        functools.partial(fold_kernel, count),
        out_shape=(jax.ShapeDtypeStruct(form, jnp.bfloat16),) * count,
        in_specs=[pl.BlockSpec(memory_space=pltpu.SMEM)] + [VMEM] * (len(pieces) + 2),
        out_specs=(VMEM,) * count,
        scratch_shapes=[
            pltpu.VMEM((rows, depth, rank), jnp.bfloat16),
            pltpu.VMEM((rank, depth), jnp.bfloat16),
            pltpu.VMEM((rows, rank, rank), jnp.float32),
        ],
        compiler_params=pltpu.CompilerParams(vmem_limit_bytes=limit),
        cost_estimate=pl.CostEstimate(
            flops=rows * depth * rank * rank, bytes_accessed=8 << 20, transcendentals=0
        ),
        name="fold",
    )(meta, *pieces, omega2t, omega3)


def weigh_kernel(omega1, out, rows, sems):
    here = lax.rem(lax.div(lax.axis_index("slab"), CORES), SIDE_Z)
    copies = []
    for chunk in range(CHUNKS):
        for step in range(SIDE_Z):
            there = lax.rem(here - step + SIDE_Z, SIDE_Z)
            copies.append(
                pltpu.make_async_copy(
                    omega1.at[:, there, :, chunk], rows.at[chunk, step], sems.at[chunk, step]
                )
            )
            copies[-1].start()
    for copy in copies:
        copy.wait()
    out[...] = rows[...].reshape(-1, rows.shape[-1]).T


def weigh(omega1):
    height, rank = omega1.shape
    lines = height // (SIDE_Y * SIDE_Z * CORES * CHUNKS)
    return pl.pallas_call(
        weigh_kernel,
        out_shape=jax.ShapeDtypeStruct((rank, height), omega1.dtype),
        in_specs=[pl.BlockSpec(memory_space=pltpu.HBM)],
        out_specs=VMEM,
        scratch_shapes=[
            pltpu.VMEM((CHUNKS, SIDE_Z, SIDE_Y, CORES, lines, rank), omega1.dtype),
            pltpu.SemaphoreType.DMA((CHUNKS, SIDE_Z)),
        ],
        compiler_params=pltpu.CompilerParams(vmem_limit_bytes=STAGE_LIMIT),
        name="weigh",
    )(omega1.reshape(SIDE_Y, SIDE_Z, CORES, CHUNKS, lines, rank))


def join_kernel(*refs):
    rows = refs[0].shape[1]
    for number, piece in enumerate(refs[:-1]):
        refs[-1][:, number * rows : (number + 1) * rows] = piece[...]


def join(pieces):
    height, rows = pieces[0].shape[:2]
    form = (height, rows * len(pieces)) + pieces[0].shape[2:]
    return pl.pallas_call(
        join_kernel,
        out_shape=jax.ShapeDtypeStruct(form, pieces[0].dtype),
        in_specs=[VMEM] * len(pieces),
        out_specs=VMEM,
        compiler_params=pltpu.CompilerParams(vmem_limit_bytes=STAGE_LIMIT),
        name="join",
    )(*pieces)


def split_kernel(whole, *pieces):
    rows = pieces[0].shape[1]
    for number, piece in enumerate(pieces):
        piece[...] = whole[:, number * rows : (number + 1) * rows]


def split(whole, count):
    form = (whole.shape[0], whole.shape[1] // count) + whole.shape[2:]
    return pl.pallas_call(
        split_kernel,
        out_shape=(jax.ShapeDtypeStruct(form, whole.dtype),) * count,
        in_specs=[VMEM],
        out_specs=(VMEM,) * count,
        compiler_params=pltpu.CompilerParams(vmem_limit_bytes=STAGE_LIMIT),
        name="split",
    )(whole)


def core_kernel(chunk, plan, has_sum, *refs):
    arrived, refs = refs[: len(plan)], refs[len(plan) :]
    weights, before = refs[0], refs[1] if has_sum else None
    out, wide = refs[-2:]
    rank = weights.shape[0]
    strip = arrived[0].shape[-2]
    depth = wide.shape[0] // strip
    for steps, piece in zip(plan, arrived):
        size = piece.shape[0] * ROWS
        for order, step in enumerate(steps):
            start = step * size * strip
            part = piece[:, order * ROWS : (order + 1) * ROWS]
            wide[start : start + size * strip] = part.astype(jnp.float32).reshape(
                size * strip, EDGE
            )
    for second in range(0, strip, 2):
        columns = [
            wide[pl.ds(second + k, depth, stride=strip), :].astype(jnp.bfloat16) for k in range(2)
        ]
        total = jnp.dot(
            weights[:, chunk * depth : (chunk + 1) * depth],
            jnp.concatenate(columns, axis=1),
            preferred_element_type=jnp.float32,
        )
        for k in range(2):
            rows = pl.ds(second + k, rank, stride=strip)
            term = total[:, k * EDGE : (k + 1) * EDGE]
            out[rows, :] = term + before[rows, :] if has_sum else term


def core(chunk, plan, arrived, weights, before=None):
    rank, depth = weights.shape
    strip = arrived[0].shape[-2]
    has_sum = before is not None
    return pl.pallas_call(
        functools.partial(core_kernel, chunk, plan, has_sum),
        out_shape=jax.ShapeDtypeStruct((rank * strip, EDGE), jnp.float32),
        in_specs=[VMEM] * (len(arrived) + 1 + has_sum),
        out_specs=VMEM,
        scratch_shapes=[pltpu.VMEM((depth // CHUNKS * strip, EDGE), jnp.float32)],
        compiler_params=pltpu.CompilerParams(vmem_limit_bytes=24 << 20),
        cost_estimate=pl.CostEstimate(
            flops=2 * depth // CHUNKS * rank * strip * EDGE,
            bytes_accessed=4 << 20,
            transcendentals=0,
        ),
        name="core",
    )(*arrived, weights, *([before] if has_sum else []))


def along_z(step):
    def slab(y, z, core):
        return (y * SIDE_Z + z) * CORES + core

    return [
        (slab(y, z, core), slab(y, (z + step) % SIDE_Z, core))
        for y in range(SIDE_Y)
        for z in range(SIDE_Z)
        for core in range(CORES)
    ]


def planes(groups):
    return [
        [
            ((y * SIDE_Z + z) * CORES + core) * groups + group
            for y in range(SIDE_Y)
            for core in range(CORES)
            for group in range(groups)
        ]
        for z in range(SIDE_Z)
    ]


def local(slabs, groups, blocks, coords, counts, omega1, omega2, omega3):
    me = lax.axis_index("grp")
    own = blocks[0]
    facts = jnp.concatenate([coords[0, 0].reshape(-1), counts[0]])

    def shift(value, step):
        return lax.ppermute(value, "grp", [(i, (i + step) % groups) for i in range(groups)])

    pieces = []
    for chunk in range(CHUNKS):
        pieces.append([])
        for step in range(groups):
            row = (chunk * groups + lax.rem(me + step, groups)) * ROWS
            piece = lax.dynamic_slice_in_dim(own, row, ROWS, 1)
            pieces[chunk].append(shift(piece, step) if step else piece)
    meta = jnp.stack([facts] + [shift(facts, step) for step in range(1, groups)])
    omega2t = omega2.T

    def leave(value, step):
        return lax.ppermute(value, "slab", along_z(step))

    def spread(value):
        return lax.all_to_all(
            value, ("slab", "grp"), 0, 0, axis_index_groups=planes(groups), tiled=True
        )

    def flat(value):
        return value.reshape((-1,) + value.shape[3:])

    (last,) = fold(meta, pieces[0], omega2t, stage(omega3), FOLD_LIMIT[0], 1, slabs, groups)
    last = spread(flat(last))
    first = fold(meta, pieces[1], omega2t, omega3, FOLD_LIMIT[1], SIDE_Z, slabs, groups)
    first = [flat(part) for part in first]
    for step in LEAVE:
        first[step] = leave(first[step], step)
    last = list(split(last, SIDE_Z))
    for step in LEAVE:
        last[step] = leave(last[step], step)
    first = join(first)
    first = spread(first)
    weights = weigh(omega1)
    plan = tuple((step,) for step in range(SIDE_Z))
    flat_core = core(0, plan, last, weights)
    flat_core = core(1, (tuple(range(SIDE_Z)),), [first], weights, flat_core)
    return flat_core.reshape(omega1.shape[1], -1, EDGE)


def solution(mesh):
    in_specs = (
        P("grp", None, "slab", None, None),
        P("grp", "slab", None, None),
        P("grp", "slab"),
        P(),
        P(),
        P(),
    )
    out_specs = P(None, "slab", "grp")
    slabs, groups = mesh.shape["slab"], mesh.shape["grp"]

    def body(*args):
        return local(slabs, groups, *args)

    return jax.shard_map(body, mesh=mesh, in_specs=in_specs, out_specs=out_specs, check_vma=False)
```

profile of v0, /device:TPU:1, one launch (start us, length us, event | category | flops | bytes accessed | tf_op | source)
XLA Modules:
  0.0 147.5 jit_solution(415262813532396166)
XLA Ops:
  0.0 2.7 %dynamic-slice_bitcast_fusion = (bf16[4,2,128,128]{3,2,1,0:T(8,128)(2,1)}, bf16[4,2,128,128]{3,2,1,0:T(8,128)(2,1)}, bf16[4,2,128,128]{3,2,1,0:T(8,128)(2,1)S(1)...) fusion(bf16[1,4,16,128,128]{4,3,2,1,0:T(8,128)(2,1)} %param.6, ...), kind=kLoop, calls=%fused_computation | loop fusion | bytes 4194336 | tf_op jit(solution)/shard_map/dynamic_slice | solution.py:291
  2.7 2.0 %collective-permute-start.13 = (bf16[4,2,128,128]{3,2,1,0:T(8,128)(2,1)}, bf16[4,2,128,128]{3,2,1,0:T(8,128)(2,1)S(1)}, u32[]{:S(2)}, u32[]{:S(2)}) collective-permute-start(bf16[4,2,128,128]{3,2,1,0:T(8,128)(2,1)} %get-tuple-element.38), channel_id=1, source_target_pairs={{0,1},{1,2},{2,3},{3,0},{4,5},{5,6},{6,7},{7,4},{8,9},{9,10},{10,1... | collective-permute-start | bytes 786440 | tf_op jit(solution)/shard_map/ppermute | solution.py:284
  4.8 2.5 %collective-permute-start.14 = (bf16[4,2,128,128]{3,2,1,0:T(8,128)(2,1)}, bf16[4,2,128,128]{3,2,1,0:T(8,128)(2,1)S(1)}, u32[]{:S(2)}, u32[]{:S(2)}) collective-permute-start(bf16[4,2,128,128]{3,2,1,0:T(8,128)(2,1)} %get-tuple-element.44), channel_id=1, source_target_pairs={{0,2},{1,3},{2,0},{3,1},{4,6},{5,7},{6,4},{7,5},{8,10},{9,11},{10,... | collective-permute-start | bytes 786440 | tf_op jit(solution)/shard_map/ppermute | solution.py:284
  7.2 1.2 collective-permute-start.15
  8.4 0.1 copy.9
  8.5 0.1 reshape_squeeze.3
  9.2 0.1 pad_add_fusion.1
  9.3 0.3 collective-permute-start
  9.6 0.9 collective-permute-start.1
  10.5 2.9 %copy.10 = bf16[2048,512]{0,1:T(8,128)(2,1)S(1)} copy(bf16[2048,512]{1,0:T(8,128)(2,1)} %param.10) | data formatting | bytes 4194304 | tf_op args[4]
  13.4 0.0 copy-start.1
  13.4 1.6 %copy-done.1 = bf16[2048,512]{1,0:T(8,128)(2,1)S(1)} copy-done((bf16[2048,512]{1,0:T(8,128)(2,1)S(1)}, bf16[2048,512]{1,0:T(8,128)(2,1)}, u32[]{:S(2)}) %copy-start.1) | copy-done | bytes 2097176
  15.0 0.1 stage.1.refs_5_
  15.2 0.1 fusion
  15.2 0.2 collective-permute-done
  15.5 3.6 %collective-permute-start.2 = (s32[9]{0:T(128)S(1)}, s32[9]{0:T(128)S(1)}, u32[]{:S(2)}, u32[]{:S(2)}) collective-permute-start(s32[9]{0:T(128)S(1)} %pad_add_fusion.1), channel_id=1, source_target_pairs={{0,3},{1,0},{2,1},{3,2},{4,7},{5,4},{6,5},{7,6},{8,11},{9,8},{10,9... | collective-permute-start | bytes 116 | tf_op jit(solution)/shard_map/ppermute | solution.py:284
  19.1 0.0 collective-permute-done.1
  19.1 0.7 collective-permute-done.2
  19.8 0.0 collective-permute-done.13.refs_1_
  19.8 0.0 collective-permute-done.15.refs_3_
  19.8 4.6 %fold.3 = bf16[4,2,4,16,8,128]{5,4,3,2,1,0:T(8,128)(2,1)} custom-call(s32[4,9]{1,0:T(4,128)S(1)} %pad_add_fusion.meta, bf16[4,2,128,128]{3,2,1,0:T(8,128)(2,1)S(1)} %get-tuple-element.39.refs_0_, bf16[4,2,128,128]{3,2,1,0:T(8,128)(2,1)S(1)} %collective-permute-done.13.refs_1_, bf16[4,2,128,128]{3,2,1,0:T(8,128)(2,1)S(1)} %collective-permute-done.14.refs_2_, ...), custom_call_target="tpu_custom_call" | custom-call | flops 1073741824 | bytes 8388608 | tf_op jit(solution)/shard_map/fold/pallas_call | solution.py:115
  24.4 10.9 %all-to-all-start.1 = ((bf16[32,16,8,128]{3,2,1,0:T(8,128)(2,1)}), bf16[32,16,8,128]{3,2,1,0:T(8,128)(2,1)S(1)}, u32[]{:S(2)}, u32[]{:S(2)}) async-start(bf16[32,16,8,128]{3,2,1,0:T(8,128)(2,1)} %bitcast.23), calls=%async_computation.1 | async-start | bytes 2097152 | tf_op jit(solution)/shard_map/all_to_all | solution.py:300
  35.4 1.4 collective-permute-start.3
  36.8 2.4 %collective-permute-start.4 = (bf16[4,2,128,128]{3,2,1,0:T(8,128)(2,1)S(1)}, bf16[4,2,128,128]{3,2,1,0:T(8,128)(2,1)S(1)}, u32[]{:S(2)}, u32[]{:S(2)}) collective-permute-start(bf16[4,2,128,128]{3,2,1,0:T(8,128)(2,1)S(1)} %copy-done.5), channel_id=1, source_target_pairs={{0,2},{1,3},{2,0},{3,1},{4,6},{5,7},{6,4},{7,5},{8,10},{9,11},{10,... | collective-permute-start | bytes 786440 | tf_op jit(solution)/shard_map/ppermute | solution.py:284
  39.2 1.2 collective-permute-start.5
  40.4 15.2 %collective-permute-done.3.refs_1_ = bf16[4,2,128,128]{3,2,1,0:T(8,128)(2,1)S(1)} collective-permute-done((bf16[4,2,128,128]{3,2,1,0:T(8,128)(2,1)S(1)}, bf16[4,2,128,128]{3,2,1,0:T(8,128)(2,1)S(1)}, u32[]{:S(2)}, u32[]{:S(2)}) %collective-permute-start.3) | collective-permute-done | bytes 262176 | tf_op jit(solution)/shard_map/ppermute | solution.py:284
  55.5 5.9 %collective-permute-done.4.refs_2_ = bf16[4,2,128,128]{3,2,1,0:T(8,128)(2,1)S(1)} collective-permute-done((bf16[4,2,128,128]{3,2,1,0:T(8,128)(2,1)S(1)}, bf16[4,2,128,128]{3,2,1,0:T(8,128)(2,1)S(1)}, u32[]{:S(2)}, u32[]{:S(2)}) %collective-permute-start.4) | collective-permute-done | bytes 262176 | tf_op jit(solution)/shard_map/ppermute | solution.py:284
  61.5 0.0 collective-permute-done.5.refs_3_
  61.5 0.7 copy-done.8
  62.2 0.1 copy-done.9
  62.3 6.5 %fold.2 = (bf16[4,2,4,2,8,128]{5,4,3,2,1,0:T(8,128)(2,1)}, bf16[4,2,4,2,8,128]{5,4,3,2,1,0:T(8,128)(2,1)}, bf16[4,2,4,2,8,128]{5,4,3,2,1,0:T(8,128)(2,1)}, bf16[...) custom-call(s32[4,9]{1,0:T(4,128)} %copy-done.4, ...), custom_call_target="tpu_custom_call" | custom-call | flops 1073741824 | bytes 8388608 | tf_op jit(solution)/shard_map/fold/pallas_call | solution.py:115
  68.8 5.7 %collective-permute-start.10 = (bf16[32,2,8,128]{3,2,1,0:T(8,128)(2,1)}, bf16[32,2,8,128]{3,2,1,0:T(8,128)(2,1)S(1)}, u32[]{:S(2)}, u32[]{:S(2)}) collective-permute-start(bf16[32,2,8,128]{3,2,1,0:T(8,128)(2,1)} %bitcast.49), channel_id=1, source_target_pairs={{0,40},{4,44},{8,48},{12,52},{16,56},{20,60},{24,0},{28,4},{32,8},... | collective-permute-start | bytes 393224 | tf_op jit(solution)/shard_map/ppermute | solution.py:297
  74.5 1.2 collective-permute-start.11
  75.6 0.3 collective-permute-start.12
  75.9 1.2 collective-permute-start.6
  77.1 1.4 collective-permute-start.7
  78.5 0.0 collective-permute-done.10.refs_5_
  78.5 6.7 %collective-permute-start.8 = (bf16[32,2,8,128]{3,2,1,0:T(8,128)(2,1)}, bf16[32,2,8,128]{3,2,1,0:T(8,128)(2,1)S(1)}, u32[]{:S(2)}, u32[]{:S(2)}) collective-permute-start(bf16[32,2,8,128]{3,2,1,0:T(8,128)(2,1)} %bitcast.44), channel_id=1, source_target_pairs={{0,24},{4,28},{8,32},{12,36},{16,40},{20,44},{24,48},{28,52},{32,5... | collective-permute-start | bytes 393224 | tf_op jit(solution)/shard_map/ppermute | solution.py:297
  85.2 2.9 %collective-permute-done.11.refs_6_ = bf16[32,2,8,128]{3,2,1,0:T(8,128)(2,1)S(1)} collective-permute-done((bf16[32,2,8,128]{3,2,1,0:T(8,128)(2,1)}, bf16[32,2,8,128]{3,2,1,0:T(8,128)(2,1)S(1)}, u32[]{:S(2)}, u32[]{:S(2)}) %collective-permute-start.11) | collective-permute-done | bytes 131104 | tf_op jit(solution)/shard_map/ppermute | solution.py:297
  88.2 2.0 %collective-permute-start.9 = (bf16[32,2,8,128]{3,2,1,0:T(8,128)(2,1)}, bf16[32,2,8,128]{3,2,1,0:T(8,128)(2,1)S(1)}, u32[]{:S(2)}, u32[]{:S(2)}) collective-permute-start(bf16[32,2,8,128]{3,2,1,0:T(8,128)(2,1)} %bitcast.43), channel_id=1, source_target_pairs={{0,32},{4,36},{8,40},{12,44},{16,48},{20,52},{24,56},{28,60},{32,0... | collective-permute-start | bytes 393224 | tf_op jit(solution)/shard_map/ppermute | solution.py:297
  90.1 1.5 %collective-permute-done.12.refs_7_ = bf16[32,2,8,128]{3,2,1,0:T(8,128)(2,1)S(1)} collective-permute-done((bf16[32,2,8,128]{3,2,1,0:T(8,128)(2,1)}, bf16[32,2,8,128]{3,2,1,0:T(8,128)(2,1)S(1)}, u32[]{:S(2)}, u32[]{:S(2)}) %collective-permute-start.12) | collective-permute-done | bytes 131104 | tf_op jit(solution)/shard_map/ppermute | solution.py:297
  91.6 0.0 collective-permute-done.7.refs_2_
  91.6 0.1 collective-permute-done.8.refs_3_
  91.8 10.5 %collective-permute-done.9.refs_4_ = bf16[32,2,8,128]{3,2,1,0:T(8,128)(2,1)S(1)} collective-permute-done((bf16[32,2,8,128]{3,2,1,0:T(8,128)(2,1)}, bf16[32,2,8,128]{3,2,1,0:T(8,128)(2,1)S(1)}, u32[]{:S(2)}, u32[]{:S(2)}) %collective-permute-start.9) | collective-permute-done | bytes 131104 | tf_op jit(solution)/shard_map/ppermute | solution.py:297
  102.2 0.9 copy-done.3
  103.1 1.1 join.1
  104.2 7.6 %all-to-all-start = ((bf16[32,16,8,128]{3,2,1,0:T(8,128)(2,1)}), bf16[32,16,8,128]{3,2,1,0:T(8,128)(2,1)}, u32[]{:S(2)}, u32[]{:S(2)}) async-start(bf16[32,16,8,128]{3,2,1,0:T(8,128)(2,1)} %join.1), calls=%async_computation | async-start | bytes 2097152 | tf_op jit(solution)/shard_map/all_to_all | solution.py:300
  111.8 0.1 split.1
  111.9 0.1 collective-permute-start.16
  112.0 2.0 %collective-permute-start.17 = (bf16[32,2,8,128]{3,2,1,0:T(8,128)(2,1)S(1)}, bf16[32,2,8,128]{3,2,1,0:T(8,128)(2,1)S(1)}, u32[]{:S(2)}, u32[]{:S(2)}) collective-permute-start(bf16[32,2,8,128]{3,2,1,0:T(8,128)(2,1)S(1)} %get-tuple-element.31), channel_id=1, source_target_pairs={{0,16},{4,20},{8,24},{12,28},{16,32},{20,36},{24,40},{28,44},{32,4... | collective-permute-start | bytes 393224 | tf_op jit(solution)/shard_map/ppermute | solution.py:297
  114.0 4.7 %collective-permute-start.18 = (bf16[32,2,8,128]{3,2,1,0:T(8,128)(2,1)S(1)}, bf16[32,2,8,128]{3,2,1,0:T(8,128)(2,1)S(1)}, u32[]{:S(2)}, u32[]{:S(2)}) collective-permute-start(bf16[32,2,8,128]{3,2,1,0:T(8,128)(2,1)S(1)} %get-tuple-element.32), channel_id=1, source_target_pairs={{0,24},{4,28},{8,32},{12,36},{16,40},{20,44},{24,48},{28,52},{32,5... | collective-permute-start | bytes 393224 | tf_op jit(solution)/shard_map/ppermute | solution.py:297
  118.8 0.8 collective-permute-start.19
  119.6 3.4 %collective-permute-start.20 = (bf16[32,2,8,128]{3,2,1,0:T(8,128)(2,1)S(1)}, bf16[32,2,8,128]{3,2,1,0:T(8,128)(2,1)S(1)}, u32[]{:S(2)}, u32[]{:S(2)}) collective-permute-start(bf16[32,2,8,128]{3,2,1,0:T(8,128)(2,1)S(1)} %get-tuple-element.34), channel_id=1, source_target_pairs={{0,40},{4,44},{8,48},{12,52},{16,56},{20,60},{24,0},{28,4},{32,8},... | collective-permute-start | bytes 393224 | tf_op jit(solution)/shard_map/ppermute | solution.py:297
  123.1 0.0 collective-permute-done.16.refs_1_
  123.1 1.7 %collective-permute-start.21 = (bf16[32,2,8,128]{3,2,1,0:T(8,128)(2,1)S(1)}, bf16[32,2,8,128]{3,2,1,0:T(8,128)(2,1)S(1)}, u32[]{:S(2)}, u32[]{:S(2)}) collective-permute-start(bf16[32,2,8,128]{3,2,1,0:T(8,128)(2,1)S(1)} %get-tuple-element.35), channel_id=1, source_target_pairs={{0,48},{4,52},{8,56},{12,60},{16,0},{20,4},{24,8},{28,12},{32,16},... | collective-permute-start | bytes 393224 | tf_op jit(solution)/shard_map/ppermute | solution.py:297
  124.8 0.0 collective-permute-done.17.refs_2_
  124.8 3.0 %collective-permute-start.22 = (bf16[32,2,8,128]{3,2,1,0:T(8,128)(2,1)S(1)}, bf16[32,2,8,128]{3,2,1,0:T(8,128)(2,1)S(1)}, u32[]{:S(2)}, u32[]{:S(2)}) collective-permute-start(bf16[32,2,8,128]{3,2,1,0:T(8,128)(2,1)S(1)} %get-tuple-element.36), channel_id=1, source_target_pairs={{0,56},{4,60},{8,0},{12,4},{16,8},{20,12},{24,16},{28,20},{32,24},... | collective-permute-start | bytes 393224 | tf_op jit(solution)/shard_map/ppermute | solution.py:297
  127.8 0.7 weigh.1.refs_8_.refs_1_
  128.6 12.0 %collective-permute-done.18.refs_3_ = bf16[32,2,8,128]{3,2,1,0:T(8,128)(2,1)S(1)} collective-permute-done((bf16[32,2,8,128]{3,2,1,0:T(8,128)(2,1)S(1)}, bf16[32,2,8,128]{3,2,1,0:T(8,128)(2,1)S(1)}, u32[]{:S(2)}, u32[]{:S(2)}) %collective-permute-start.18) | collective-permute-done | bytes 131104 | tf_op jit(solution)/shard_map/ppermute | solution.py:297
  140.5 0.0 collective-permute-done.19.refs_4_
  140.5 2.2 %collective-permute-done.21.refs_6_ = bf16[32,2,8,128]{3,2,1,0:T(8,128)(2,1)S(1)} collective-permute-done((bf16[32,2,8,128]{3,2,1,0:T(8,128)(2,1)S(1)}, bf16[32,2,8,128]{3,2,1,0:T(8,128)(2,1)S(1)}, u32[]{:S(2)}, u32[]{:S(2)}) %collective-permute-start.21) | collective-permute-done | bytes 131104 | tf_op jit(solution)/shard_map/ppermute | solution.py:297
  142.7 0.0 collective-permute-done.22.refs_7_
  142.7 1.0 core.2.refs_2_
  143.7 3.8 %core.3 = f32[4096,128]{1,0:T(8,128)} custom-call(bf16[32,16,8,128]{3,2,1,0:T(8,128)(2,1)} %all-to-all-done.refs_0_, bf16[512,1024]{1,0:T(8,128)(2,1)S(1)} %weigh.1.refs_8_.refs_1_, f32[4096,128]{1,0:T(8,128)S(1)} %core.2.refs_2_), custom_call_target="tpu_custom_call" | custom-call | flops 536870912 | bytes 4194304 | tf_op jit(solution)/shard_map/core/pallas_call | solution.py:238
  (23 shorter events, 0.1 us)
Async XLA Ops:
  0.0 8.4 %copy-start.10 = (s32[1,1,4,2]{2,3,1,0:T(2,128)S(1)}, s32[1,1,4,2]{2,3,1,0:T(2,128)}, u32[]{:S(2)}) copy-start(s32[1,1,4,2]{2,3,1,0:T(2,128)} %param.7) | copy-start | bytes 100
  2.7 17.1 %collective-permute-start.13 = (bf16[4,2,128,128]{3,2,1,0:T(8,128)(2,1)}, bf16[4,2,128,128]{3,2,1,0:T(8,128)(2,1)S(1)}, u32[]{:S(2)}, u32[]{:S(2)}) collective-permute-start(bf16[4,2,128,128]{3,2,1,0:T(8,128)(2,1)} %get-tuple-element.38), channel_id=1, source_target_pairs={{0,1},{1,2},{2,3},{3,0},{4,5},{5,6},{6,7},{7,4},{8,9},{9,10},{10,1... | collective-permute-start | bytes 786440 | tf_op jit(solution)/shard_map/ppermute | solution.py:284
  4.8 15.1 %collective-permute-start.14 = (bf16[4,2,128,128]{3,2,1,0:T(8,128)(2,1)}, bf16[4,2,128,128]{3,2,1,0:T(8,128)(2,1)S(1)}, u32[]{:S(2)}, u32[]{:S(2)}) collective-permute-start(bf16[4,2,128,128]{3,2,1,0:T(8,128)(2,1)} %get-tuple-element.44), channel_id=1, source_target_pairs={{0,2},{1,3},{2,0},{3,1},{4,6},{5,7},{6,4},{7,5},{8,10},{9,11},{10,... | collective-permute-start | bytes 786440 | tf_op jit(solution)/shard_map/ppermute | solution.py:284
  7.2 12.6 %collective-permute-start.15 = (bf16[4,2,128,128]{3,2,1,0:T(8,128)(2,1)}, bf16[4,2,128,128]{3,2,1,0:T(8,128)(2,1)S(1)}, u32[]{:S(2)}, u32[]{:S(2)}) collective-permute-start(bf16[4,2,128,128]{3,2,1,0:T(8,128)(2,1)} %get-tuple-element.37), channel_id=1, source_target_pairs={{0,3},{1,0},{2,1},{3,2},{4,7},{5,4},{6,5},{7,6},{8,11},{9,8},{10,9... | collective-permute-start | bytes 786440 | tf_op jit(solution)/shard_map/ppermute | solution.py:284
  9.3 6.2 %collective-permute-start = (s32[9]{0:T(128)S(1)}, s32[9]{0:T(128)S(1)}, u32[]{:S(2)}, u32[]{:S(2)}) collective-permute-start(s32[9]{0:T(128)S(1)} %pad_add_fusion.1), channel_id=1, source_target_pairs={{0,1},{1,2},{2,3},{3,0},{4,5},{5,6},{6,7},{7,4},{8,9},{9,10},{10,1... | collective-permute-start | bytes 116 | tf_op jit(solution)/shard_map/ppermute | solution.py:284
  9.6 9.5 %collective-permute-start.1 = (s32[9]{0:T(128)S(1)}, s32[9]{0:T(128)S(1)}, u32[]{:S(2)}, u32[]{:S(2)}) collective-permute-start(s32[9]{0:T(128)S(1)} %pad_add_fusion.1), channel_id=1, source_target_pairs={{0,2},{1,3},{2,0},{3,1},{4,6},{5,7},{6,4},{7,5},{8,10},{9,11},{10,... | collective-permute-start | bytes 116 | tf_op jit(solution)/shard_map/ppermute | solution.py:284
  13.4 1.6 %copy-start.1 = (bf16[2048,512]{1,0:T(8,128)(2,1)S(1)}, bf16[2048,512]{1,0:T(8,128)(2,1)}, u32[]{:S(2)}) copy-start(bf16[2048,512]{1,0:T(8,128)(2,1)} %omega.1) | copy-start | bytes 6291460
  15.0 4.8 %copy-start = (bf16[2048,512]{0,1:T(8,128)(2,1)}, bf16[2048,512]{0,1:T(8,128)(2,1)S(1)}, u32[]{:S(2)}) copy-start(bf16[2048,512]{0,1:T(8,128)(2,1)S(1)} %copy.10) | copy-start | bytes 6291460
  15.5 4.3 %collective-permute-start.2 = (s32[9]{0:T(128)S(1)}, s32[9]{0:T(128)S(1)}, u32[]{:S(2)}, u32[]{:S(2)}) collective-permute-start(s32[9]{0:T(128)S(1)} %pad_add_fusion.1), channel_id=1, source_target_pairs={{0,3},{1,0},{2,1},{3,2},{4,7},{5,4},{6,5},{7,6},{8,11},{9,8},{10,9... | collective-permute-start | bytes 116 | tf_op jit(solution)/shard_map/ppermute | solution.py:284
  19.8 4.6 %copy-start.4 = (s32[4,9]{1,0:T(4,128)}, s32[4,9]{1,0:T(4,128)S(1)}, u32[]{:S(2)}) copy-start(s32[4,9]{1,0:T(4,128)S(1)} %pad_add_fusion.meta) | copy-start | bytes 436
  24.4 11.0 %copy-start.6 = (bf16[4,2,128,128]{3,2,1,0:T(8,128)(2,1)S(1)}, bf16[4,2,128,128]{3,2,1,0:T(8,128)(2,1)}, u32[]{:S(2)}) copy-start(bf16[4,2,128,128]{3,2,1,0:T(8,128)(2,1)} %get-tuple-element.42) | copy-start | bytes 786436
  24.4 12.4 %copy-start.5 = (bf16[4,2,128,128]{3,2,1,0:T(8,128)(2,1)S(1)}, bf16[4,2,128,128]{3,2,1,0:T(8,128)(2,1)}, u32[]{:S(2)}) copy-start(bf16[4,2,128,128]{3,2,1,0:T(8,128)(2,1)} %get-tuple-element.41) | copy-start | bytes 786436
  24.4 79.8 %all-to-all-start.1 = ((bf16[32,16,8,128]{3,2,1,0:T(8,128)(2,1)}), bf16[32,16,8,128]{3,2,1,0:T(8,128)(2,1)S(1)}, u32[]{:S(2)}, u32[]{:S(2)}) async-start(bf16[32,16,8,128]{3,2,1,0:T(8,128)(2,1)} %bitcast.23), calls=%async_computation.1 | async-start | bytes 2097152 | tf_op jit(solution)/shard_map/all_to_all | solution.py:300
  35.4 20.2 %collective-permute-start.3 = (bf16[4,2,128,128]{3,2,1,0:T(8,128)(2,1)S(1)}, bf16[4,2,128,128]{3,2,1,0:T(8,128)(2,1)S(1)}, u32[]{:S(2)}, u32[]{:S(2)}) collective-permute-start(bf16[4,2,128,128]{3,2,1,0:T(8,128)(2,1)S(1)} %copy-done.6), channel_id=1, source_target_pairs={{0,1},{1,2},{2,3},{3,0},{4,5},{5,6},{6,7},{7,4},{8,9},{9,10},{10,1... | collective-permute-start | bytes 786440 | tf_op jit(solution)/shard_map/ppermute | solution.py:284
  36.8 24.6 %collective-permute-start.4 = (bf16[4,2,128,128]{3,2,1,0:T(8,128)(2,1)S(1)}, bf16[4,2,128,128]{3,2,1,0:T(8,128)(2,1)S(1)}, u32[]{:S(2)}, u32[]{:S(2)}) collective-permute-start(bf16[4,2,128,128]{3,2,1,0:T(8,128)(2,1)S(1)} %copy-done.5), channel_id=1, source_target_pairs={{0,2},{1,3},{2,0},{3,1},{4,6},{5,7},{6,4},{7,5},{8,10},{9,11},{10,... | collective-permute-start | bytes 786440 | tf_op jit(solution)/shard_map/ppermute | solution.py:284
  39.2 22.3 %collective-permute-start.5 = (bf16[4,2,128,128]{3,2,1,0:T(8,128)(2,1)S(1)}, bf16[4,2,128,128]{3,2,1,0:T(8,128)(2,1)S(1)}, u32[]{:S(2)}, u32[]{:S(2)}) collective-permute-start(bf16[4,2,128,128]{3,2,1,0:T(8,128)(2,1)S(1)} %get-tuple-element.40), channel_id=1, source_target_pairs={{0,3},{1,0},{2,1},{3,2},{4,7},{5,4},{6,5},{7,6},{8,11},{9,8},{10,9... | collective-permute-start | bytes 786440 | tf_op jit(solution)/shard_map/ppermute | solution.py:284
  55.5 5.9 %copy-start.7 = (bf16[4,2,128,128]{3,2,1,0:T(8,128)(2,1)}, bf16[4,2,128,128]{3,2,1,0:T(8,128)(2,1)S(1)}, u32[]{:S(2)}) copy-start(bf16[4,2,128,128]{3,2,1,0:T(8,128)(2,1)S(1)} %collective-permute-done.3.refs_1_) | copy-start | bytes 786436
  61.5 0.7 copy-start.8
  61.5 0.8 copy-start.9
  68.8 9.7 %collective-permute-start.10 = (bf16[32,2,8,128]{3,2,1,0:T(8,128)(2,1)}, bf16[32,2,8,128]{3,2,1,0:T(8,128)(2,1)S(1)}, u32[]{:S(2)}, u32[]{:S(2)}) collective-permute-start(bf16[32,2,8,128]{3,2,1,0:T(8,128)(2,1)} %bitcast.49), channel_id=1, source_target_pairs={{0,40},{4,44},{8,48},{12,52},{16,56},{20,60},{24,0},{28,4},{32,8},... | collective-permute-start | bytes 393224 | tf_op jit(solution)/shard_map/ppermute | solution.py:297
  74.5 13.7 %collective-permute-start.11 = (bf16[32,2,8,128]{3,2,1,0:T(8,128)(2,1)}, bf16[32,2,8,128]{3,2,1,0:T(8,128)(2,1)S(1)}, u32[]{:S(2)}, u32[]{:S(2)}) collective-permute-start(bf16[32,2,8,128]{3,2,1,0:T(8,128)(2,1)} %bitcast.48), channel_id=1, source_target_pairs={{0,48},{4,52},{8,56},{12,60},{16,0},{20,4},{24,8},{28,12},{32,16},... | collective-permute-start | bytes 393224 | tf_op jit(solution)/shard_map/ppermute | solution.py:297
  75.6 16.0 %collective-permute-start.12 = (bf16[32,2,8,128]{3,2,1,0:T(8,128)(2,1)}, bf16[32,2,8,128]{3,2,1,0:T(8,128)(2,1)S(1)}, u32[]{:S(2)}, u32[]{:S(2)}) collective-permute-start(bf16[32,2,8,128]{3,2,1,0:T(8,128)(2,1)} %bitcast.47), channel_id=1, source_target_pairs={{0,56},{4,60},{8,0},{12,4},{16,8},{20,12},{24,16},{28,20},{32,24},... | collective-permute-start | bytes 393224 | tf_op jit(solution)/shard_map/ppermute | solution.py:297
  75.9 15.7 %collective-permute-start.6 = (bf16[32,2,8,128]{3,2,1,0:T(8,128)(2,1)}, bf16[32,2,8,128]{3,2,1,0:T(8,128)(2,1)S(1)}, u32[]{:S(2)}, u32[]{:S(2)}) collective-permute-start(bf16[32,2,8,128]{3,2,1,0:T(8,128)(2,1)} %bitcast.46), channel_id=1, source_target_pairs={{0,8},{4,12},{8,16},{12,20},{16,24},{20,28},{24,32},{28,36},{32,40... | collective-permute-start | bytes 393224 | tf_op jit(solution)/shard_map/ppermute | solution.py:297
  77.1 14.5 %collective-permute-start.7 = (bf16[32,2,8,128]{3,2,1,0:T(8,128)(2,1)}, bf16[32,2,8,128]{3,2,1,0:T(8,128)(2,1)S(1)}, u32[]{:S(2)}, u32[]{:S(2)}) collective-permute-start(bf16[32,2,8,128]{3,2,1,0:T(8,128)(2,1)} %bitcast.45), channel_id=1, source_target_pairs={{0,16},{4,20},{8,24},{12,28},{16,32},{20,36},{24,40},{28,44},{32,4... | collective-permute-start | bytes 393224 | tf_op jit(solution)/shard_map/ppermute | solution.py:297
  78.5 13.3 %collective-permute-start.8 = (bf16[32,2,8,128]{3,2,1,0:T(8,128)(2,1)}, bf16[32,2,8,128]{3,2,1,0:T(8,128)(2,1)S(1)}, u32[]{:S(2)}, u32[]{:S(2)}) collective-permute-start(bf16[32,2,8,128]{3,2,1,0:T(8,128)(2,1)} %bitcast.44), channel_id=1, source_target_pairs={{0,24},{4,28},{8,32},{12,36},{16,40},{20,44},{24,48},{28,52},{32,5... | collective-permute-start | bytes 393224 | tf_op jit(solution)/shard_map/ppermute | solution.py:297
  88.2 14.1 %collective-permute-start.9 = (bf16[32,2,8,128]{3,2,1,0:T(8,128)(2,1)}, bf16[32,2,8,128]{3,2,1,0:T(8,128)(2,1)S(1)}, u32[]{:S(2)}, u32[]{:S(2)}) collective-permute-start(bf16[32,2,8,128]{3,2,1,0:T(8,128)(2,1)} %bitcast.43), channel_id=1, source_target_pairs={{0,32},{4,36},{8,40},{12,44},{16,48},{20,52},{24,56},{28,60},{32,0... | collective-permute-start | bytes 393224 | tf_op jit(solution)/shard_map/ppermute | solution.py:297
  102.2 0.9 copy-start.3
  104.2 23.6 %copy-start.2 = (bf16[1024,512]{1,0:T(8,128)(2,1)S(1)}, bf16[1024,512]{1,0:T(8,128)(2,1)}, u32[]{:S(2)}) copy-start(bf16[1024,512]{1,0:T(8,128)(2,1)} %param.9) | copy-start | bytes 3145732
  104.2 39.4 %all-to-all-start = ((bf16[32,16,8,128]{3,2,1,0:T(8,128)(2,1)}), bf16[32,16,8,128]{3,2,1,0:T(8,128)(2,1)}, u32[]{:S(2)}, u32[]{:S(2)}) async-start(bf16[32,16,8,128]{3,2,1,0:T(8,128)(2,1)} %join.1), calls=%async_computation | async-start | bytes 2097152 | tf_op jit(solution)/shard_map/all_to_all | solution.py:300
  111.9 11.1 %collective-permute-start.16 = (bf16[32,2,8,128]{3,2,1,0:T(8,128)(2,1)S(1)}, bf16[32,2,8,128]{3,2,1,0:T(8,128)(2,1)S(1)}, u32[]{:S(2)}, u32[]{:S(2)}) collective-permute-start(bf16[32,2,8,128]{3,2,1,0:T(8,128)(2,1)S(1)} %get-tuple-element.30), channel_id=1, source_target_pairs={{0,8},{4,12},{8,16},{12,20},{16,24},{20,28},{24,32},{28,36},{32,40... | collective-permute-start | bytes 393224 | tf_op jit(solution)/shard_map/ppermute | solution.py:297
  112.0 12.8 %collective-permute-start.17 = (bf16[32,2,8,128]{3,2,1,0:T(8,128)(2,1)S(1)}, bf16[32,2,8,128]{3,2,1,0:T(8,128)(2,1)S(1)}, u32[]{:S(2)}, u32[]{:S(2)}) collective-permute-start(bf16[32,2,8,128]{3,2,1,0:T(8,128)(2,1)S(1)} %get-tuple-element.31), channel_id=1, source_target_pairs={{0,16},{4,20},{8,24},{12,28},{16,32},{20,36},{24,40},{28,44},{32,4... | collective-permute-start | bytes 393224 | tf_op jit(solution)/shard_map/ppermute | solution.py:297
  114.0 26.5 %collective-permute-start.18 = (bf16[32,2,8,128]{3,2,1,0:T(8,128)(2,1)S(1)}, bf16[32,2,8,128]{3,2,1,0:T(8,128)(2,1)S(1)}, u32[]{:S(2)}, u32[]{:S(2)}) collective-permute-start(bf16[32,2,8,128]{3,2,1,0:T(8,128)(2,1)S(1)} %get-tuple-element.32), channel_id=1, source_target_pairs={{0,24},{4,28},{8,32},{12,36},{16,40},{20,44},{24,48},{28,52},{32,5... | collective-permute-start | bytes 393224 | tf_op jit(solution)/shard_map/ppermute | solution.py:297
  118.8 21.8 %collective-permute-start.19 = (bf16[32,2,8,128]{3,2,1,0:T(8,128)(2,1)S(1)}, bf16[32,2,8,128]{3,2,1,0:T(8,128)(2,1)S(1)}, u32[]{:S(2)}, u32[]{:S(2)}) collective-permute-start(bf16[32,2,8,128]{3,2,1,0:T(8,128)(2,1)S(1)} %get-tuple-element.33), channel_id=1, source_target_pairs={{0,32},{4,36},{8,40},{12,44},{16,48},{20,52},{24,56},{28,60},{32,0... | collective-permute-start | bytes 393224 | tf_op jit(solution)/shard_map/ppermute | solution.py:297
  119.6 20.9 %collective-permute-start.20 = (bf16[32,2,8,128]{3,2,1,0:T(8,128)(2,1)S(1)}, bf16[32,2,8,128]{3,2,1,0:T(8,128)(2,1)S(1)}, u32[]{:S(2)}, u32[]{:S(2)}) collective-permute-start(bf16[32,2,8,128]{3,2,1,0:T(8,128)(2,1)S(1)} %get-tuple-element.34), channel_id=1, source_target_pairs={{0,40},{4,44},{8,48},{12,52},{16,56},{20,60},{24,0},{28,4},{32,8},... | collective-permute-start | bytes 393224 | tf_op jit(solution)/shard_map/ppermute | solution.py:297
  123.1 19.6 %collective-permute-start.21 = (bf16[32,2,8,128]{3,2,1,0:T(8,128)(2,1)S(1)}, bf16[32,2,8,128]{3,2,1,0:T(8,128)(2,1)S(1)}, u32[]{:S(2)}, u32[]{:S(2)}) collective-permute-start(bf16[32,2,8,128]{3,2,1,0:T(8,128)(2,1)S(1)} %get-tuple-element.35), channel_id=1, source_target_pairs={{0,48},{4,52},{8,56},{12,60},{16,0},{20,4},{24,8},{28,12},{32,16},... | collective-permute-start | bytes 393224 | tf_op jit(solution)/shard_map/ppermute | solution.py:297
  124.8 17.9 %collective-permute-start.22 = (bf16[32,2,8,128]{3,2,1,0:T(8,128)(2,1)S(1)}, bf16[32,2,8,128]{3,2,1,0:T(8,128)(2,1)S(1)}, u32[]{:S(2)}, u32[]{:S(2)}) collective-permute-start(bf16[32,2,8,128]{3,2,1,0:T(8,128)(2,1)S(1)} %get-tuple-element.36), channel_id=1, source_target_pairs={{0,56},{4,60},{8,0},{12,4},{16,8},{20,12},{24,16},{28,20},{32,24},... | collective-permute-start | bytes 393224 | tf_op jit(solution)/shard_map/ppermute | solution.py:297
where the time goes:
time: 149 us; the launch traced here: 147 us
  starting transfers between devices  68.3 us (46%)
  waiting for transfers between devices  51.2 us (34%)
  Pallas kernels  17.8 us (12%)
  local copies, waits for them, and re-layouts  9.15 us (6%)
    ppermute x14, starting transfers between devices, leave(): return lax.ppermute(value, 'slab', along_z(step))  34.3 us
    ppermute x14, waiting for transfers between devices, leave(): return lax.ppermute(value, 'slab', along_z(step))  29.2 us
    ppermute x9, waiting for transfers between devices, shift(): lax.ppermute(value, 'grp', [(i, (i + step) % groups) for i in range(group...  22 us
    all_to_all x2, starting transfers between devices, spread(): lax.all_to_all(value, ('slab', 'grp'), 0, 0, axis_index_groups=planes(gro...  18.5 us
    ppermute x9, starting transfers between devices, shift(): lax.ppermute(value, 'grp', [(i, (i + step) % groups) for i in range(group...  15.4 us
    pallas_call x2, Pallas kernels, fold(): pl.pallas_call(functools.partial(fold_kernel, count), out_shape=(jax.Shap...  11.1 us
    unnamed x24, local copies, waits for them, and re-layouts  6.34 us
    pallas_call x2, Pallas kernels, core(): pl.pallas_call(functools.partial(core_kernel, chunk, plan, has_sum), out_...  4.74 us
  transfers between devices with their start and end apart: 25, of which 10 were waited for; matrix products, arithmetic and copies ran while one was open for 2% of the time, Pallas kernels for 6%

commit v1 on v0

--- a/solution.py
+++ b/solution.py
@@ -11,7 +11,7 @@
 EDGE = 128
 SIDE_Y, SIDE_Z, CORES = 4, 8, 2
 CHUNKS, ROWS = 2, 2
-LEAVE = (4, 3, 5, 2, 6, 1, 7)
+LEAVE = (1, 7, 3, 5, 4, 2, 6)
 STAGE_LIMIT = 16 << 20
 FOLD_LIMIT = (40 << 20, 56 << 20)
 VMEM = pl.BlockSpec(memory_space=pltpu.VMEM)
@@ -201,17 +201,15 @@
     )(whole)
 
 
-def core_kernel(chunk, plan, has_sum, *refs):
-    arrived, refs = refs[: len(plan)], refs[len(plan) :]
-    weights, before = refs[0], refs[1] if has_sum else None
-    out, wide = refs[-2:]
+def core_kernel(plan, *refs):
+    arrived, (weights, out, wide) = refs[:-3], refs[-3:]
     rank = weights.shape[0]
+    depth = weights.shape[1]
     strip = arrived[0].shape[-2]
-    depth = wide.shape[0] // strip
-    for steps, piece in zip(plan, arrived):
+    for (chunk, steps), piece in zip(plan, arrived):
         size = piece.shape[0] * ROWS
         for order, step in enumerate(steps):
-            start = step * size * strip
+            start = (chunk * SIDE_Z + step) * size * strip
             part = piece[:, order * ROWS : (order + 1) * ROWS]
             wide[start : start + size * strip] = part.astype(jnp.float32).reshape(
                 size * strip, EDGE
@@ -221,34 +219,28 @@
             wide[pl.ds(second + k, depth, stride=strip), :].astype(jnp.bfloat16) for k in range(2)
         ]
         total = jnp.dot(
-            weights[:, chunk * depth : (chunk + 1) * depth],
-            jnp.concatenate(columns, axis=1),
-            preferred_element_type=jnp.float32,
+            weights[...], jnp.concatenate(columns, axis=1), preferred_element_type=jnp.float32
         )
         for k in range(2):
-            rows = pl.ds(second + k, rank, stride=strip)
-            term = total[:, k * EDGE : (k + 1) * EDGE]
-            out[rows, :] = term + before[rows, :] if has_sum else term
-
-
-def core(chunk, plan, arrived, weights, before=None):
+            out[pl.ds(second + k, rank, stride=strip), :] = total[:, k * EDGE : (k + 1) * EDGE]
+
+
+def core(plan, arrived, weights):
     rank, depth = weights.shape
     strip = arrived[0].shape[-2]
-    has_sum = before is not None
-    return pl.pallas_call(
-        functools.partial(core_kernel, chunk, plan, has_sum),
+    flat = pl.pallas_call(
+        functools.partial(core_kernel, plan),
         out_shape=jax.ShapeDtypeStruct((rank * strip, EDGE), jnp.float32),
-        in_specs=[VMEM] * (len(arrived) + 1 + has_sum),
+        in_specs=[VMEM] * (len(arrived) + 1),
         out_specs=VMEM,
-        scratch_shapes=[pltpu.VMEM((depth // CHUNKS * strip, EDGE), jnp.float32)],
+        scratch_shapes=[pltpu.VMEM((depth * strip, EDGE), jnp.float32)],
         compiler_params=pltpu.CompilerParams(vmem_limit_bytes=24 << 20),
         cost_estimate=pl.CostEstimate(
-            flops=2 * depth // CHUNKS * rank * strip * EDGE,
-            bytes_accessed=4 << 20,
-            transcendentals=0,
+            flops=2 * depth * rank * strip * EDGE, bytes_accessed=4 << 20, transcendentals=0
         ),
         name="core",
-    )(*arrived, weights, *([before] if has_sum else []))
+    )(*arrived, weights)
+    return flat.reshape(rank, strip, EDGE)
 
 
 def along_z(step):
@@ -316,10 +308,8 @@
     first = join(first)
     first = spread(first)
     weights = weigh(omega1)
-    plan = tuple((step,) for step in range(SIDE_Z))
-    flat_core = core(0, plan, last, weights)
-    flat_core = core(1, (tuple(range(SIDE_Z)),), [first], weights, flat_core)
-    return flat_core.reshape(omega1.shape[1], -1, EDGE)
+    plan = [(1, tuple(range(SIDE_Z)))] + [(0, (step,)) for step in range(SIDE_Z)]
+    return core(tuple(plan), [first] + last, weights)
 
 
 def solution(mesh):

time: 149 us -> 151 us (1.013)
  waiting for transfers between devices: 51.2 us -> 61.7 us
  starting transfers between devices: 68.3 us -> 60.8 us
    ppermute x14, waiting for transfers between devices: 29.2 us -> 36.3 us  [leave(): return lax.ppermute(value, 'slab', along_z(step))]
    ppermute x14, starting transfers between devices: 34.3 us -> 29.7 us  [leave(): return lax.ppermute(value, 'slab', along_z(step))]
    ppermute x9, waiting for transfers between devices: 22 us -> 24.8 us  [shift(): lax.ppermute(value, 'grp', [(i, (i + step) % groups) for i in range(group...]
    all_to_all x2, starting transfers between devices: 18.5 us -> 16.2 us  [spread(): lax.all_to_all(value, ('slab', 'grp'), 0, 0, axis_index_groups=planes(gro...]
    pallas_call x2 -> x1, Pallas kernels: 4.74 us -> 4.11 us  [core(): pl.pallas_call(functools.partial(core_kernel, plan), out_shape=jax.ShapeD...]
  transfers between devices with their start and end apart: 25 -> 25, of which waited for: 10 -> 13; matrix products, arithmetic and copies ran while one was open for 2% -> 2% of each run, Pallas kernels for 6% -> 6%
where the time goes in v1:
time: 151 us
  waiting for transfers between devices  61.7 us (41%)
  starting transfers between devices  60.8 us (40%)
  Pallas kernels  18.1 us (12%)
  local copies, waits for them, and re-layouts  9.15 us (6%)
    ppermute x14, waiting for transfers between devices, leave(): return lax.ppermute(value, 'slab', along_z(step))  36.3 us
    ppermute x14, starting transfers between devices, leave(): return lax.ppermute(value, 'slab', along_z(step))  29.7 us
    ppermute x9, waiting for transfers between devices, shift(): lax.ppermute(value, 'grp', [(i, (i + step) % groups) for i in range(group...  24.8 us
    all_to_all x2, starting transfers between devices, spread(): lax.all_to_all(value, ('slab', 'grp'), 0, 0, axis_index_groups=planes(gro...  16.2 us
    ppermute x9, starting transfers between devices, shift(): lax.ppermute(value, 'grp', [(i, (i + step) % groups) for i in range(group...  14.9 us
    pallas_call x2, Pallas kernels, fold(): pl.pallas_call(functools.partial(fold_kernel, count), out_shape=(jax.Shap...  11 us
    unnamed x24, local copies, waits for them, and re-layouts  6.34 us
    pallas_call x1, Pallas kernels, core(): pl.pallas_call(functools.partial(core_kernel, plan), out_shape=jax.ShapeD...  4.11 us
  transfers between devices with their start and end apart: 25, of which 13 were waited for; matrix products, arithmetic and copies ran while one was open for 2% of the time, Pallas kernels for 6%

profile of v1, /device:TPU:1, one launch (start us, length us, event | category | flops | bytes accessed | tf_op | source)
XLA Modules:
  0.0 150.6 jit_solution(4334981026547765188)
XLA Ops:
  0.0 2.7 %dynamic-slice_bitcast_fusion = (bf16[4,2,128,128]{3,2,1,0:T(8,128)(2,1)}, bf16[4,2,128,128]{3,2,1,0:T(8,128)(2,1)}, bf16[4,2,128,128]{3,2,1,0:T(8,128)(2,1)S(1)...) fusion(bf16[1,4,16,128,128]{4,3,2,1,0:T(8,128)(2,1)} %param.6, ...), kind=kLoop, calls=%fused_computation | loop fusion | bytes 4194336 | tf_op jit(solution)/shard_map/dynamic_slice | solution.py:283
  2.7 2.0 %collective-permute-start.13 = (bf16[4,2,128,128]{3,2,1,0:T(8,128)(2,1)}, bf16[4,2,128,128]{3,2,1,0:T(8,128)(2,1)S(1)}, u32[]{:S(2)}, u32[]{:S(2)}) collective-permute-start(bf16[4,2,128,128]{3,2,1,0:T(8,128)(2,1)} %get-tuple-element.38), channel_id=1, source_target_pairs={{0,1},{1,2},{2,3},{3,0},{4,5},{5,6},{6,7},{7,4},{8,9},{9,10},{10,1... | collective-permute-start | bytes 786440 | tf_op jit(solution)/shard_map/ppermute | solution.py:276
  4.8 2.5 %collective-permute-start.14 = (bf16[4,2,128,128]{3,2,1,0:T(8,128)(2,1)}, bf16[4,2,128,128]{3,2,1,0:T(8,128)(2,1)S(1)}, u32[]{:S(2)}, u32[]{:S(2)}) collective-permute-start(bf16[4,2,128,128]{3,2,1,0:T(8,128)(2,1)} %get-tuple-element.44), channel_id=1, source_target_pairs={{0,2},{1,3},{2,0},{3,1},{4,6},{5,7},{6,4},{7,5},{8,10},{9,11},{10,... | collective-permute-start | bytes 786440 | tf_op jit(solution)/shard_map/ppermute | solution.py:276
  7.2 1.2 collective-permute-start.15
  9.0 0.1 copy.9
  9.1 0.1 reshape_squeeze.3
  9.2 0.1 pad_add_fusion.1
  9.3 0.0 collective-permute-start.2
  9.3 2.1 %collective-permute-start.1 = (s32[9]{0:T(128)S(1)}, s32[9]{0:T(128)S(1)}, u32[]{:S(2)}, u32[]{:S(2)}) collective-permute-start(s32[9]{0:T(128)S(1)} %pad_add_fusion.1), channel_id=1, source_target_pairs={{0,2},{1,3},{2,0},{3,1},{4,6},{5,7},{6,4},{7,5},{8,10},{9,11},{10,... | collective-permute-start | bytes 116 | tf_op jit(solution)/shard_map/ppermute | solution.py:276
  11.4 2.9 %copy.10 = bf16[2048,512]{0,1:T(8,128)(2,1)S(1)} copy(bf16[2048,512]{1,0:T(8,128)(2,1)} %param.10) | data formatting | bytes 4194304 | tf_op args[4]
  14.3 0.0 copy-start.1
  14.3 1.6 %copy-done.1 = bf16[2048,512]{1,0:T(8,128)(2,1)S(1)} copy-done((bf16[2048,512]{1,0:T(8,128)(2,1)S(1)}, bf16[2048,512]{1,0:T(8,128)(2,1)}, u32[]{:S(2)}) %copy-start.1) | copy-done | bytes 2097176
  15.9 0.1 stage.1.refs_5_
  16.1 0.1 fusion
  16.2 1.6 %collective-permute-done.2 = s32[9]{0:T(128)S(1)} collective-permute-done((s32[9]{0:T(128)S(1)}, s32[9]{0:T(128)S(1)}, u32[]{:S(2)}, u32[]{:S(2)}) %collective-permute-start.2) | collective-permute-done | bytes 68 | tf_op jit(solution)/shard_map/ppermute | solution.py:276
  17.8 2.1 %collective-permute-start = (s32[9]{0:T(128)S(1)}, s32[9]{0:T(128)S(1)}, u32[]{:S(2)}, u32[]{:S(2)}) collective-permute-start(s32[9]{0:T(128)S(1)} %pad_add_fusion.1), channel_id=1, source_target_pairs={{0,1},{1,2},{2,3},{3,0},{4,5},{5,6},{6,7},{7,4},{8,9},{9,10},{10,1... | collective-permute-start | bytes 116 | tf_op jit(solution)/shard_map/ppermute | solution.py:276
  19.9 0.0 collective-permute-done.1
  19.9 2.1 %collective-permute-done = s32[9]{0:T(128)S(1)} collective-permute-done((s32[9]{0:T(128)S(1)}, s32[9]{0:T(128)S(1)}, u32[]{:S(2)}, u32[]{:S(2)}) %collective-permute-start) | collective-permute-done | bytes 68 | tf_op jit(solution)/shard_map/ppermute | solution.py:276
  22.1 0.0 collective-permute-done.14.refs_2_
  22.1 0.0 collective-permute-done.15.refs_3_
  22.1 4.6 %fold.3 = bf16[4,2,4,16,8,128]{5,4,3,2,1,0:T(8,128)(2,1)} custom-call(s32[4,9]{1,0:T(4,128)S(1)} %pad_add_fusion.meta, bf16[4,2,128,128]{3,2,1,0:T(8,128)(2,1)S(1)} %get-tuple-element.39.refs_0_, bf16[4,2,128,128]{3,2,1,0:T(8,128)(2,1)S(1)} %collective-permute-done.13.refs_1_, bf16[4,2,128,128]{3,2,1,0:T(8,128)(2,1)S(1)} %collective-permute-done.14.refs_2_, ...), custom_call_target="tpu_custom_call" | custom-call | flops 1073741824 | bytes 8388608 | tf_op jit(solution)/shard_map/fold/pallas_call | solution.py:115
  26.7 9.6 %all-to-all-start.1 = ((bf16[32,16,8,128]{3,2,1,0:T(8,128)(2,1)}), bf16[32,16,8,128]{3,2,1,0:T(8,128)(2,1)S(1)}, u32[]{:S(2)}, u32[]{:S(2)}) async-start(bf16[32,16,8,128]{3,2,1,0:T(8,128)(2,1)} %bitcast.22), calls=%async_computation.1 | async-start | bytes 2097152 | tf_op jit(solution)/shard_map/all_to_all | solution.py:292
  36.3 1.4 collective-permute-start.3
  37.8 2.4 %collective-permute-start.4 = (bf16[4,2,128,128]{3,2,1,0:T(8,128)(2,1)S(1)}, bf16[4,2,128,128]{3,2,1,0:T(8,128)(2,1)S(1)}, u32[]{:S(2)}, u32[]{:S(2)}) collective-permute-start(bf16[4,2,128,128]{3,2,1,0:T(8,128)(2,1)S(1)} %copy-done.5), channel_id=1, source_target_pairs={{0,2},{1,3},{2,0},{3,1},{4,6},{5,7},{6,4},{7,5},{8,10},{9,11},{10,... | collective-permute-start | bytes 786440 | tf_op jit(solution)/shard_map/ppermute | solution.py:276
  40.2 1.2 collective-permute-start.5
  41.4 15.2 %collective-permute-done.3.refs_1_ = bf16[4,2,128,128]{3,2,1,0:T(8,128)(2,1)S(1)} collective-permute-done((bf16[4,2,128,128]{3,2,1,0:T(8,128)(2,1)S(1)}, bf16[4,2,128,128]{3,2,1,0:T(8,128)(2,1)S(1)}, u32[]{:S(2)}, u32[]{:S(2)}) %collective-permute-start.3) | collective-permute-done | bytes 262176 | tf_op jit(solution)/shard_map/ppermute | solution.py:276
  56.5 5.9 %collective-permute-done.4.refs_2_ = bf16[4,2,128,128]{3,2,1,0:T(8,128)(2,1)S(1)} collective-permute-done((bf16[4,2,128,128]{3,2,1,0:T(8,128)(2,1)S(1)}, bf16[4,2,128,128]{3,2,1,0:T(8,128)(2,1)S(1)}, u32[]{:S(2)}, u32[]{:S(2)}) %collective-permute-start.4) | collective-permute-done | bytes 262176 | tf_op jit(solution)/shard_map/ppermute | solution.py:276
  62.4 0.0 collective-permute-done.5.refs_3_
  62.4 0.7 copy-done.8
  63.1 0.1 copy-done.9
  63.2 6.5 %fold.2 = (bf16[4,2,4,2,8,128]{5,4,3,2,1,0:T(8,128)(2,1)}, bf16[4,2,4,2,8,128]{5,4,3,2,1,0:T(8,128)(2,1)}, bf16[4,2,4,2,8,128]{5,4,3,2,1,0:T(8,128)(2,1)}, bf16[...) custom-call(s32[4,9]{1,0:T(4,128)} %copy-done.4, ...), custom_call_target="tpu_custom_call" | custom-call | flops 1073741824 | bytes 8388608 | tf_op jit(solution)/shard_map/fold/pallas_call | solution.py:115
  69.7 1.6 %collective-permute-start.6 = (bf16[32,2,8,128]{3,2,1,0:T(8,128)(2,1)}, bf16[32,2,8,128]{3,2,1,0:T(8,128)(2,1)S(1)}, u32[]{:S(2)}, u32[]{:S(2)}) collective-permute-start(bf16[32,2,8,128]{3,2,1,0:T(8,128)(2,1)} %bitcast.49), channel_id=1, source_target_pairs={{0,8},{4,12},{8,16},{12,20},{16,24},{20,28},{24,32},{28,36},{32,40... | collective-permute-start | bytes 393224 | tf_op jit(solution)/shard_map/ppermute | solution.py:289
  71.3 3.2 %collective-permute-start.7 = (bf16[32,2,8,128]{3,2,1,0:T(8,128)(2,1)}, bf16[32,2,8,128]{3,2,1,0:T(8,128)(2,1)S(1)}, u32[]{:S(2)}, u32[]{:S(2)}) collective-permute-start(bf16[32,2,8,128]{3,2,1,0:T(8,128)(2,1)} %bitcast.48), channel_id=1, source_target_pairs={{0,16},{4,20},{8,24},{12,28},{16,32},{20,36},{24,40},{28,44},{32,4... | collective-permute-start | bytes 393224 | tf_op jit(solution)/shard_map/ppermute | solution.py:289
  74.5 3.8 %collective-permute-start.8 = (bf16[32,2,8,128]{3,2,1,0:T(8,128)(2,1)}, bf16[32,2,8,128]{3,2,1,0:T(8,128)(2,1)S(1)}, u32[]{:S(2)}, u32[]{:S(2)}) collective-permute-start(bf16[32,2,8,128]{3,2,1,0:T(8,128)(2,1)} %bitcast.47), channel_id=1, source_target_pairs={{0,24},{4,28},{8,32},{12,36},{16,40},{20,44},{24,48},{28,52},{32,5... | collective-permute-start | bytes 393224 | tf_op jit(solution)/shard_map/ppermute | solution.py:289
  78.3 0.0 collective-permute-start.9
  78.3 4.3 %collective-permute-start.10 = (bf16[32,2,8,128]{3,2,1,0:T(8,128)(2,1)}, bf16[32,2,8,128]{3,2,1,0:T(8,128)(2,1)S(1)}, u32[]{:S(2)}, u32[]{:S(2)}) collective-permute-start(bf16[32,2,8,128]{3,2,1,0:T(8,128)(2,1)} %bitcast.45), channel_id=1, source_target_pairs={{0,40},{4,44},{8,48},{12,52},{16,56},{20,60},{24,0},{28,4},{32,8},... | collective-permute-start | bytes 393224 | tf_op jit(solution)/shard_map/ppermute | solution.py:289
  82.6 2.2 %collective-permute-start.11 = (bf16[32,2,8,128]{3,2,1,0:T(8,128)(2,1)}, bf16[32,2,8,128]{3,2,1,0:T(8,128)(2,1)S(1)}, u32[]{:S(2)}, u32[]{:S(2)}) collective-permute-start(bf16[32,2,8,128]{3,2,1,0:T(8,128)(2,1)} %bitcast.44), channel_id=1, source_target_pairs={{0,48},{4,52},{8,56},{12,60},{16,0},{20,4},{24,8},{28,12},{32,16},... | collective-permute-start | bytes 393224 | tf_op jit(solution)/shard_map/ppermute | solution.py:289
  84.7 0.0 collective-permute-done.7.refs_2_
  84.7 2.3 %collective-permute-start.12 = (bf16[32,2,8,128]{3,2,1,0:T(8,128)(2,1)}, bf16[32,2,8,128]{3,2,1,0:T(8,128)(2,1)S(1)}, u32[]{:S(2)}, u32[]{:S(2)}) collective-permute-start(bf16[32,2,8,128]{3,2,1,0:T(8,128)(2,1)} %bitcast.43), channel_id=1, source_target_pairs={{0,56},{4,60},{8,0},{12,4},{16,8},{20,12},{24,16},{28,20},{32,24},... | collective-permute-start | bytes 393224 | tf_op jit(solution)/shard_map/ppermute | solution.py:289
  87.0 9.3 %collective-permute-done.8.refs_3_ = bf16[32,2,8,128]{3,2,1,0:T(8,128)(2,1)S(1)} collective-permute-done((bf16[32,2,8,128]{3,2,1,0:T(8,128)(2,1)}, bf16[32,2,8,128]{3,2,1,0:T(8,128)(2,1)S(1)}, u32[]{:S(2)}, u32[]{:S(2)}) %collective-permute-start.8) | collective-permute-done | bytes 131104 | tf_op jit(solution)/shard_map/ppermute | solution.py:289
  96.3 0.0 collective-permute-done.9.refs_4_
  96.3 0.0 collective-permute-done.10.refs_5_
  96.3 5.7 %collective-permute-done.11.refs_6_ = bf16[32,2,8,128]{3,2,1,0:T(8,128)(2,1)S(1)} collective-permute-done((bf16[32,2,8,128]{3,2,1,0:T(8,128)(2,1)}, bf16[32,2,8,128]{3,2,1,0:T(8,128)(2,1)S(1)}, u32[]{:S(2)}, u32[]{:S(2)}) %collective-permute-start.11) | collective-permute-done | bytes 131104 | tf_op jit(solution)/shard_map/ppermute | solution.py:289
  102.1 1.4 collective-permute-done.12.refs_7_
  103.5 0.9 copy-done.3
  104.4 1.1 join.1
  105.5 0.0 all-to-all-done.1.whole
  105.5 6.5 %all-to-all-start = ((bf16[32,16,8,128]{3,2,1,0:T(8,128)(2,1)}), bf16[32,16,8,128]{3,2,1,0:T(8,128)(2,1)S(1)}, u32[]{:S(2)}, u32[]{:S(2)}) async-start(bf16[32,16,8,128]{3,2,1,0:T(8,128)(2,1)} %join.1), calls=%async_computation | async-start | bytes 2097152 | tf_op jit(solution)/shard_map/all_to_all | solution.py:292
  112.0 0.9 split.1
  113.0 3.1 %collective-permute-start.16 = (bf16[32,2,8,128]{3,2,1,0:T(8,128)(2,1)S(1)}, bf16[32,2,8,128]{3,2,1,0:T(8,128)(2,1)S(1)}, u32[]{:S(2)}, u32[]{:S(2)}) collective-permute-start(bf16[32,2,8,128]{3,2,1,0:T(8,128)(2,1)S(1)} %get-tuple-element.30), channel_id=1, source_target_pairs={{0,8},{4,12},{8,16},{12,20},{16,24},{20,28},{24,32},{28,36},{32,40... | collective-permute-start | bytes 393224 | tf_op jit(solution)/shard_map/ppermute | solution.py:289
  116.1 1.1 collective-permute-start.17
  117.2 0.3 collective-permute-start.18
  117.5 4.2 %collective-permute-start.19 = (bf16[32,2,8,128]{3,2,1,0:T(8,128)(2,1)}, bf16[32,2,8,128]{3,2,1,0:T(8,128)(2,1)}, u32[]{:S(2)}, u32[]{:S(2)}) collective-permute-start(bf16[32,2,8,128]{3,2,1,0:T(8,128)(2,1)} %get-tuple-element.33), channel_id=1, source_target_pairs={{0,32},{4,36},{8,40},{12,44},{16,48},{20,52},{24,56},{28,60},{32,0... | collective-permute-start | bytes 393224 | tf_op jit(solution)/shard_map/ppermute | solution.py:289
  121.7 1.4 collective-permute-start.20
  123.1 0.0 collective-permute-done.16.refs_2_
  123.1 2.3 %collective-permute-start.21 = (bf16[32,2,8,128]{3,2,1,0:T(8,128)(2,1)}, bf16[32,2,8,128]{3,2,1,0:T(8,128)(2,1)}, u32[]{:S(2)}, u32[]{:S(2)}) collective-permute-start(bf16[32,2,8,128]{3,2,1,0:T(8,128)(2,1)} %get-tuple-element.35), channel_id=1, source_target_pairs={{0,48},{4,52},{8,56},{12,60},{16,0},{20,4},{24,8},{28,12},{32,16},... | collective-permute-start | bytes 393224 | tf_op jit(solution)/shard_map/ppermute | solution.py:289
  125.4 1.5 collective-permute-done.17.refs_3_
  126.9 0.7 weigh.1.refs_9_
  127.6 0.5 all-to-all-done.refs_0_
  128.1 4.7 %collective-permute-done.18.refs_4_ = bf16[32,2,8,128]{3,2,1,0:T(8,128)(2,1)} collective-permute-done((bf16[32,2,8,128]{3,2,1,0:T(8,128)(2,1)}, bf16[32,2,8,128]{3,2,1,0:T(8,128)(2,1)}, u32[]{:S(2)}, u32[]{:S(2)}) %collective-permute-start.18) | collective-permute-done | bytes 131104 | tf_op jit(solution)/shard_map/ppermute | solution.py:289
  132.9 4.8 %collective-permute-done.19.refs_5_ = bf16[32,2,8,128]{3,2,1,0:T(8,128)(2,1)} collective-permute-done((bf16[32,2,8,128]{3,2,1,0:T(8,128)(2,1)}, bf16[32,2,8,128]{3,2,1,0:T(8,128)(2,1)}, u32[]{:S(2)}, u32[]{:S(2)}) %collective-permute-start.19) | collective-permute-done | bytes 131104 | tf_op jit(solution)/shard_map/ppermute | solution.py:289
  137.7 6.4 %collective-permute-done.21.refs_7_ = bf16[32,2,8,128]{3,2,1,0:T(8,128)(2,1)} collective-permute-done((bf16[32,2,8,128]{3,2,1,0:T(8,128)(2,1)}, bf16[32,2,8,128]{3,2,1,0:T(8,128)(2,1)}, u32[]{:S(2)}, u32[]{:S(2)}) %collective-permute-start.21) | collective-permute-done | bytes 131104 | tf_op jit(solution)/shard_map/ppermute | solution.py:289
  144.1 2.4 %collective-permute-done.22.refs_8_ = bf16[32,2,8,128]{3,2,1,0:T(8,128)(2,1)} collective-permute-done((bf16[32,2,8,128]{3,2,1,0:T(8,128)(2,1)}, bf16[32,2,8,128]{3,2,1,0:T(8,128)(2,1)}, u32[]{:S(2)}, u32[]{:S(2)}) %collective-permute-start.22) | collective-permute-done | bytes 131104 | tf_op jit(solution)/shard_map/ppermute | solution.py:289
  146.5 4.1 %core.1 = f32[4096,128]{1,0:T(8,128)} custom-call(bf16[32,16,8,128]{3,2,1,0:T(8,128)(2,1)S(1)} %all-to-all-done.refs_0_, bf16[32,2,8,128]{3,2,1,0:T(8,128)(2,1)S(1)} %get-tuple-element.29.refs_1_, bf16[32,2,8,128]{3,2,1,0:T(8,128)(2,1)S(1)} %collective-permute-done.16.refs_2_, bf16[32,2,8,128]{3,2,1,0:T(8,128)(2,1)S(1)} %collective-permute-done.17.refs_3_, ...), custom_call_target="tpu_custom_call" | custom-call | flops 1073741824 | bytes 4194304 | tf_op jit(solution)/shard_map/core/pallas_call | solution.py:231
  (22 shorter events, 0.1 us)
Async XLA Ops:
  0.0 9.0 %copy-start.10 = (s32[1,1,4,2]{2,3,1,0:T(2,128)S(1)}, s32[1,1,4,2]{2,3,1,0:T(2,128)}, u32[]{:S(2)}) copy-start(s32[1,1,4,2]{2,3,1,0:T(2,128)} %param.7) | copy-start | bytes 100
  2.7 19.3 %collective-permute-start.13 = (bf16[4,2,128,128]{3,2,1,0:T(8,128)(2,1)}, bf16[4,2,128,128]{3,2,1,0:T(8,128)(2,1)S(1)}, u32[]{:S(2)}, u32[]{:S(2)}) collective-permute-start(bf16[4,2,128,128]{3,2,1,0:T(8,128)(2,1)} %get-tuple-element.38), channel_id=1, source_target_pairs={{0,1},{1,2},{2,3},{3,0},{4,5},{5,6},{6,7},{7,4},{8,9},{9,10},{10,1... | collective-permute-start | bytes 786440 | tf_op jit(solution)/shard_map/ppermute | solution.py:276
  4.8 17.3 %collective-permute-start.14 = (bf16[4,2,128,128]{3,2,1,0:T(8,128)(2,1)}, bf16[4,2,128,128]{3,2,1,0:T(8,128)(2,1)S(1)}, u32[]{:S(2)}, u32[]{:S(2)}) collective-permute-start(bf16[4,2,128,128]{3,2,1,0:T(8,128)(2,1)} %get-tuple-element.44), channel_id=1, source_target_pairs={{0,2},{1,3},{2,0},{3,1},{4,6},{5,7},{6,4},{7,5},{8,10},{9,11},{10,... | collective-permute-start | bytes 786440 | tf_op jit(solution)/shard_map/ppermute | solution.py:276
  7.2 14.9 %collective-permute-start.15 = (bf16[4,2,128,128]{3,2,1,0:T(8,128)(2,1)}, bf16[4,2,128,128]{3,2,1,0:T(8,128)(2,1)S(1)}, u32[]{:S(2)}, u32[]{:S(2)}) collective-permute-start(bf16[4,2,128,128]{3,2,1,0:T(8,128)(2,1)} %get-tuple-element.37), channel_id=1, source_target_pairs={{0,3},{1,0},{2,1},{3,2},{4,7},{5,4},{6,5},{7,6},{8,11},{9,8},{10,9... | collective-permute-start | bytes 786440 | tf_op jit(solution)/shard_map/ppermute | solution.py:276
  9.3 8.5 %collective-permute-start.2 = (s32[9]{0:T(128)S(1)}, s32[9]{0:T(128)S(1)}, u32[]{:S(2)}, u32[]{:S(2)}) collective-permute-start(s32[9]{0:T(128)S(1)} %pad_add_fusion.1), channel_id=1, source_target_pairs={{0,3},{1,0},{2,1},{3,2},{4,7},{5,4},{6,5},{7,6},{8,11},{9,8},{10,9... | collective-permute-start | bytes 116 | tf_op jit(solution)/shard_map/ppermute | solution.py:276
  9.3 10.6 %collective-permute-start.1 = (s32[9]{0:T(128)S(1)}, s32[9]{0:T(128)S(1)}, u32[]{:S(2)}, u32[]{:S(2)}) collective-permute-start(s32[9]{0:T(128)S(1)} %pad_add_fusion.1), channel_id=1, source_target_pairs={{0,2},{1,3},{2,0},{3,1},{4,6},{5,7},{6,4},{7,5},{8,10},{9,11},{10,... | collective-permute-start | bytes 116 | tf_op jit(solution)/shard_map/ppermute | solution.py:276
  14.3 1.6 %copy-start.1 = (bf16[2048,512]{1,0:T(8,128)(2,1)S(1)}, bf16[2048,512]{1,0:T(8,128)(2,1)}, u32[]{:S(2)}) copy-start(bf16[2048,512]{1,0:T(8,128)(2,1)} %omega.1) | copy-start | bytes 6291460
  15.9 6.2 %copy-start = (bf16[2048,512]{0,1:T(8,128)(2,1)}, bf16[2048,512]{0,1:T(8,128)(2,1)S(1)}, u32[]{:S(2)}) copy-start(bf16[2048,512]{0,1:T(8,128)(2,1)S(1)} %copy.10) | copy-start | bytes 6291460
  17.8 4.3 %collective-permute-start = (s32[9]{0:T(128)S(1)}, s32[9]{0:T(128)S(1)}, u32[]{:S(2)}, u32[]{:S(2)}) collective-permute-start(s32[9]{0:T(128)S(1)} %pad_add_fusion.1), channel_id=1, source_target_pairs={{0,1},{1,2},{2,3},{3,0},{4,5},{5,6},{6,7},{7,4},{8,9},{9,10},{10,1... | collective-permute-start | bytes 116 | tf_op jit(solution)/shard_map/ppermute | solution.py:276
  22.1 4.6 %copy-start.4 = (s32[4,9]{1,0:T(4,128)}, s32[4,9]{1,0:T(4,128)S(1)}, u32[]{:S(2)}) copy-start(s32[4,9]{1,0:T(4,128)S(1)} %pad_add_fusion.meta) | copy-start | bytes 436
  26.7 9.7 %copy-start.6 = (bf16[4,2,128,128]{3,2,1,0:T(8,128)(2,1)S(1)}, bf16[4,2,128,128]{3,2,1,0:T(8,128)(2,1)}, u32[]{:S(2)}) copy-start(bf16[4,2,128,128]{3,2,1,0:T(8,128)(2,1)} %get-tuple-element.42) | copy-start | bytes 786436
  26.7 11.1 %copy-start.5 = (bf16[4,2,128,128]{3,2,1,0:T(8,128)(2,1)S(1)}, bf16[4,2,128,128]{3,2,1,0:T(8,128)(2,1)}, u32[]{:S(2)}) copy-start(bf16[4,2,128,128]{3,2,1,0:T(8,128)(2,1)} %get-tuple-element.41) | copy-start | bytes 786436
  26.7 78.8 %all-to-all-start.1 = ((bf16[32,16,8,128]{3,2,1,0:T(8,128)(2,1)}), bf16[32,16,8,128]{3,2,1,0:T(8,128)(2,1)S(1)}, u32[]{:S(2)}, u32[]{:S(2)}) async-start(bf16[32,16,8,128]{3,2,1,0:T(8,128)(2,1)} %bitcast.22), calls=%async_computation.1 | async-start | bytes 2097152 | tf_op jit(solution)/shard_map/all_to_all | solution.py:292
  36.3 20.2 %collective-permute-start.3 = (bf16[4,2,128,128]{3,2,1,0:T(8,128)(2,1)S(1)}, bf16[4,2,128,128]{3,2,1,0:T(8,128)(2,1)S(1)}, u32[]{:S(2)}, u32[]{:S(2)}) collective-permute-start(bf16[4,2,128,128]{3,2,1,0:T(8,128)(2,1)S(1)} %copy-done.6), channel_id=1, source_target_pairs={{0,1},{1,2},{2,3},{3,0},{4,5},{5,6},{6,7},{7,4},{8,9},{9,10},{10,1... | collective-permute-start | bytes 786440 | tf_op jit(solution)/shard_map/ppermute | solution.py:276
  37.8 24.6 %collective-permute-start.4 = (bf16[4,2,128,128]{3,2,1,0:T(8,128)(2,1)S(1)}, bf16[4,2,128,128]{3,2,1,0:T(8,128)(2,1)S(1)}, u32[]{:S(2)}, u32[]{:S(2)}) collective-permute-start(bf16[4,2,128,128]{3,2,1,0:T(8,128)(2,1)S(1)} %copy-done.5), channel_id=1, source_target_pairs={{0,2},{1,3},{2,0},{3,1},{4,6},{5,7},{6,4},{7,5},{8,10},{9,11},{10,... | collective-permute-start | bytes 786440 | tf_op jit(solution)/shard_map/ppermute | solution.py:276
  40.2 22.3 %collective-permute-start.5 = (bf16[4,2,128,128]{3,2,1,0:T(8,128)(2,1)S(1)}, bf16[4,2,128,128]{3,2,1,0:T(8,128)(2,1)S(1)}, u32[]{:S(2)}, u32[]{:S(2)}) collective-permute-start(bf16[4,2,128,128]{3,2,1,0:T(8,128)(2,1)S(1)} %get-tuple-element.40), channel_id=1, source_target_pairs={{0,3},{1,0},{2,1},{3,2},{4,7},{5,4},{6,5},{7,6},{8,11},{9,8},{10,9... | collective-permute-start | bytes 786440 | tf_op jit(solution)/shard_map/ppermute | solution.py:276
  56.5 5.9 %copy-start.7 = (bf16[4,2,128,128]{3,2,1,0:T(8,128)(2,1)}, bf16[4,2,128,128]{3,2,1,0:T(8,128)(2,1)S(1)}, u32[]{:S(2)}) copy-start(bf16[4,2,128,128]{3,2,1,0:T(8,128)(2,1)S(1)} %collective-permute-done.3.refs_1_) | copy-start | bytes 786436
  62.4 0.7 copy-start.8
  62.4 0.8 copy-start.9
  69.7 12.8 %collective-permute-start.6 = (bf16[32,2,8,128]{3,2,1,0:T(8,128)(2,1)}, bf16[32,2,8,128]{3,2,1,0:T(8,128)(2,1)S(1)}, u32[]{:S(2)}, u32[]{:S(2)}) collective-permute-start(bf16[32,2,8,128]{3,2,1,0:T(8,128)(2,1)} %bitcast.49), channel_id=1, source_target_pairs={{0,8},{4,12},{8,16},{12,20},{16,24},{20,28},{24,32},{28,36},{32,40... | collective-permute-start | bytes 393224 | tf_op jit(solution)/shard_map/ppermute | solution.py:289
  71.3 13.4 %collective-permute-start.7 = (bf16[32,2,8,128]{3,2,1,0:T(8,128)(2,1)}, bf16[32,2,8,128]{3,2,1,0:T(8,128)(2,1)S(1)}, u32[]{:S(2)}, u32[]{:S(2)}) collective-permute-start(bf16[32,2,8,128]{3,2,1,0:T(8,128)(2,1)} %bitcast.48), channel_id=1, source_target_pairs={{0,16},{4,20},{8,24},{12,28},{16,32},{20,36},{24,40},{28,44},{32,4... | collective-permute-start | bytes 393224 | tf_op jit(solution)/shard_map/ppermute | solution.py:289
  74.5 21.8 %collective-permute-start.8 = (bf16[32,2,8,128]{3,2,1,0:T(8,128)(2,1)}, bf16[32,2,8,128]{3,2,1,0:T(8,128)(2,1)S(1)}, u32[]{:S(2)}, u32[]{:S(2)}) collective-permute-start(bf16[32,2,8,128]{3,2,1,0:T(8,128)(2,1)} %bitcast.47), channel_id=1, source_target_pairs={{0,24},{4,28},{8,32},{12,36},{16,40},{20,44},{24,48},{28,52},{32,5... | collective-permute-start | bytes 393224 | tf_op jit(solution)/shard_map/ppermute | solution.py:289
  78.3 18.1 %collective-permute-start.9 = (bf16[32,2,8,128]{3,2,1,0:T(8,128)(2,1)}, bf16[32,2,8,128]{3,2,1,0:T(8,128)(2,1)S(1)}, u32[]{:S(2)}, u32[]{:S(2)}) collective-permute-start(bf16[32,2,8,128]{3,2,1,0:T(8,128)(2,1)} %bitcast.46), channel_id=1, source_target_pairs={{0,32},{4,36},{8,40},{12,44},{16,48},{20,52},{24,56},{28,60},{32,0... | collective-permute-start | bytes 393224 | tf_op jit(solution)/shard_map/ppermute | solution.py:289
  78.3 18.1 %collective-permute-start.10 = (bf16[32,2,8,128]{3,2,1,0:T(8,128)(2,1)}, bf16[32,2,8,128]{3,2,1,0:T(8,128)(2,1)S(1)}, u32[]{:S(2)}, u32[]{:S(2)}) collective-permute-start(bf16[32,2,8,128]{3,2,1,0:T(8,128)(2,1)} %bitcast.45), channel_id=1, source_target_pairs={{0,40},{4,44},{8,48},{12,52},{16,56},{20,60},{24,0},{28,4},{32,8},... | collective-permute-start | bytes 393224 | tf_op jit(solution)/shard_map/ppermute | solution.py:289
  82.6 19.5 %collective-permute-start.11 = (bf16[32,2,8,128]{3,2,1,0:T(8,128)(2,1)}, bf16[32,2,8,128]{3,2,1,0:T(8,128)(2,1)S(1)}, u32[]{:S(2)}, u32[]{:S(2)}) collective-permute-start(bf16[32,2,8,128]{3,2,1,0:T(8,128)(2,1)} %bitcast.44), channel_id=1, source_target_pairs={{0,48},{4,52},{8,56},{12,60},{16,0},{20,4},{24,8},{28,12},{32,16},... | collective-permute-start | bytes 393224 | tf_op jit(solution)/shard_map/ppermute | solution.py:289
  84.7 18.7 %collective-permute-start.12 = (bf16[32,2,8,128]{3,2,1,0:T(8,128)(2,1)}, bf16[32,2,8,128]{3,2,1,0:T(8,128)(2,1)S(1)}, u32[]{:S(2)}, u32[]{:S(2)}) collective-permute-start(bf16[32,2,8,128]{3,2,1,0:T(8,128)(2,1)} %bitcast.43), channel_id=1, source_target_pairs={{0,56},{4,60},{8,0},{12,4},{16,8},{20,12},{24,16},{28,20},{32,24},... | collective-permute-start | bytes 393224 | tf_op jit(solution)/shard_map/ppermute | solution.py:289
  103.5 0.9 copy-start.3
  105.5 21.4 %copy-start.2 = (bf16[1024,512]{1,0:T(8,128)(2,1)S(1)}, bf16[1024,512]{1,0:T(8,128)(2,1)}, u32[]{:S(2)}) copy-start(bf16[1024,512]{1,0:T(8,128)(2,1)} %param.9) | copy-start | bytes 3145732
  105.5 22.6 %all-to-all-start = ((bf16[32,16,8,128]{3,2,1,0:T(8,128)(2,1)}), bf16[32,16,8,128]{3,2,1,0:T(8,128)(2,1)S(1)}, u32[]{:S(2)}, u32[]{:S(2)}) async-start(bf16[32,16,8,128]{3,2,1,0:T(8,128)(2,1)} %join.1), calls=%async_computation | async-start | bytes 2097152 | tf_op jit(solution)/shard_map/all_to_all | solution.py:292
  113.0 10.1 %collective-permute-start.16 = (bf16[32,2,8,128]{3,2,1,0:T(8,128)(2,1)S(1)}, bf16[32,2,8,128]{3,2,1,0:T(8,128)(2,1)S(1)}, u32[]{:S(2)}, u32[]{:S(2)}) collective-permute-start(bf16[32,2,8,128]{3,2,1,0:T(8,128)(2,1)S(1)} %get-tuple-element.30), channel_id=1, source_target_pairs={{0,8},{4,12},{8,16},{12,20},{16,24},{20,28},{24,32},{28,36},{32,40... | collective-permute-start | bytes 393224 | tf_op jit(solution)/shard_map/ppermute | solution.py:289
  116.1 10.8 %collective-permute-start.17 = (bf16[32,2,8,128]{3,2,1,0:T(8,128)(2,1)S(1)}, bf16[32,2,8,128]{3,2,1,0:T(8,128)(2,1)S(1)}, u32[]{:S(2)}, u32[]{:S(2)}) collective-permute-start(bf16[32,2,8,128]{3,2,1,0:T(8,128)(2,1)S(1)} %get-tuple-element.31), channel_id=1, source_target_pairs={{0,16},{4,20},{8,24},{12,28},{16,32},{20,36},{24,40},{28,44},{32,4... | collective-permute-start | bytes 393224 | tf_op jit(solution)/shard_map/ppermute | solution.py:289
  117.2 15.7 %collective-permute-start.18 = (bf16[32,2,8,128]{3,2,1,0:T(8,128)(2,1)}, bf16[32,2,8,128]{3,2,1,0:T(8,128)(2,1)}, u32[]{:S(2)}, u32[]{:S(2)}) collective-permute-start(bf16[32,2,8,128]{3,2,1,0:T(8,128)(2,1)} %get-tuple-element.32), channel_id=1, source_target_pairs={{0,24},{4,28},{8,32},{12,36},{16,40},{20,44},{24,48},{28,52},{32,5... | collective-permute-start | bytes 393224 | tf_op jit(solution)/shard_map/ppermute | solution.py:289
  117.5 20.2 %collective-permute-start.19 = (bf16[32,2,8,128]{3,2,1,0:T(8,128)(2,1)}, bf16[32,2,8,128]{3,2,1,0:T(8,128)(2,1)}, u32[]{:S(2)}, u32[]{:S(2)}) collective-permute-start(bf16[32,2,8,128]{3,2,1,0:T(8,128)(2,1)} %get-tuple-element.33), channel_id=1, source_target_pairs={{0,32},{4,36},{8,40},{12,44},{16,48},{20,52},{24,56},{28,60},{32,0... | collective-permute-start | bytes 393224 | tf_op jit(solution)/shard_map/ppermute | solution.py:289
  121.7 16.0 %collective-permute-start.20 = (bf16[32,2,8,128]{3,2,1,0:T(8,128)(2,1)}, bf16[32,2,8,128]{3,2,1,0:T(8,128)(2,1)}, u32[]{:S(2)}, u32[]{:S(2)}) collective-permute-start(bf16[32,2,8,128]{3,2,1,0:T(8,128)(2,1)} %get-tuple-element.34), channel_id=1, source_target_pairs={{0,40},{4,44},{8,48},{12,52},{16,56},{20,60},{24,0},{28,4},{32,8},... | collective-permute-start | bytes 393224 | tf_op jit(solution)/shard_map/ppermute | solution.py:289
  123.1 21.0 %collective-permute-start.21 = (bf16[32,2,8,128]{3,2,1,0:T(8,128)(2,1)}, bf16[32,2,8,128]{3,2,1,0:T(8,128)(2,1)}, u32[]{:S(2)}, u32[]{:S(2)}) collective-permute-start(bf16[32,2,8,128]{3,2,1,0:T(8,128)(2,1)} %get-tuple-element.35), channel_id=1, source_target_pairs={{0,48},{4,52},{8,56},{12,60},{16,0},{20,4},{24,8},{28,12},{32,16},... | collective-permute-start | bytes 393224 | tf_op jit(solution)/shard_map/ppermute | solution.py:289
  126.9 19.6 %collective-permute-start.22 = (bf16[32,2,8,128]{3,2,1,0:T(8,128)(2,1)}, bf16[32,2,8,128]{3,2,1,0:T(8,128)(2,1)}, u32[]{:S(2)}, u32[]{:S(2)}) collective-permute-start(bf16[32,2,8,128]{3,2,1,0:T(8,128)(2,1)} %get-tuple-element.36), channel_id=1, source_target_pairs={{0,56},{4,60},{8,0},{12,4},{16,8},{20,12},{24,16},{28,20},{32,24},... | collective-permute-start | bytes 393224 | tf_op jit(solution)/shard_map/ppermute | solution.py:289
